TPU v7x, 32 devices: a whole 2x2x4 slice. The times are simulated.
32 devices in a mesh: groups: 2 (over y), strip: 4 (over z), panel: 2 (over x), sub: 2 (over core).
Axes of the slice: x: 2, y: 2, z: 4, core: 2. Of those that a mesh axis runs over, the one named last changes fastest.
Arguments:
- start_block: float32 [64, 128, 256], P('groups', ('strip', 'sub'), 'panel'), parts along dimension 0, may hold values from -120 to 120, as said below
- edge_weights: float32 [16, 128, 256], P('groups', ('strip', 'sub'), 'panel'), parts along dimension 0, may hold values from 0 to 1, as said below
- mass: float32 [256, 256], P(('groups', 'strip', 'sub'), 'panel'), parts along dimension 0, may hold values from 0.5 to 2
- locked: bfloat16 [2048, 128, 256], P(('groups', 'panel'), ('strip', 'sub')), parts along dimension 0, may hold values from -4 to 4
Outputs:
- ortho: float32 [64, 128, 256], P('groups', ('strip', 'sub'), 'panel'), parts along dimension 0
- coupling: float32 [2048, 32], P(('groups', 'panel')), parts along dimension 0
- r_factor: float32 [64, 32], P('groups'), parts along dimension 0
There are 2 independent parts, one for each index of `groups`. A program takes and returns all parts, laid end to end along the dimension named above; each array names one. Nothing has to cross between parts.
Inputs may be any that keep to these rules, and one draw needn't show every extreme that they name: `start_block`: the sum of an entry's square over the block's vertices is positive for every vector. edge_weights[k + 4] at vertex (i, j) equals edge_weights[k] at vertex (i, j) - o_k for k = 0..3, and is zero where that vertex lies outside the grid; edge_weights[0..3] are positive everywhere.
All inputs are finite; a program needn't handle non-finite values.
Results may differ from a plain program's by a relative error of at most 0.003.
Values may be sent and summed in bfloat16 or wider, within the bound.
No kernel may reach another device: no remote copies, remote signals or barrier semaphores. Data moves between devices by JAX's collectives and lax.ppermute only.
A program may use at most 64 MiB of HBM per device.

v0:
```python
import math
import jax
import jax.numpy as jnp
from jax import lax
from jax.sharding import PartitionSpec as P

DEGREE = 6
CUT_LOW = 2
CUT_HIGH = 32
OFFSETS = ((0, 1), (1, 0), (1, 1), (1, -1), (0, -1), (-1, 0), (-1, -1), (-1, 1))


def with_halo(array, sides, width):
    for axis, dim in sides:
        devices, length = (lax.axis_size(axis), array.shape[dim])
        up = [(i, (i + 1) % devices) for i in range(devices - 1)]
        down = [(j, i) for i, j in up]
        last = lax.slice_in_dim(array, length - width, length, axis=dim)
        leading = lax.slice_in_dim(array, 0, width, axis=dim)
        before = lax.ppermute(last, axis, up)
        after = lax.ppermute(leading, axis, down)
        array = jnp.concatenate([before, array, after], axis=dim)
    return array


def apply_operator(vectors, edge_weights, scaling):
    scaled = scaling * vectors
    padded = with_halo(scaled, ((("strip", "sub"), 1), ("panel", 2)), 1)
    height = scaled.shape[1]
    across = scaled.shape[2]
    summed = jnp.zeros_like(scaled)
    for direction in range(8):
        step_row, step_col = OFFSETS[direction]
        beside = padded[
            :, 1 + step_row : 1 + step_row + height, 1 + step_col : 1 + step_col + across
        ]
        summed = summed + edge_weights[direction] * (scaled - beside)
    return scaling * summed


def chebyshev(start_block, edge_weights, scaling):
    centre = 0.5 * (CUT_HIGH + CUT_LOW)
    spread = 0.5 * (CUT_HIGH - CUT_LOW)
    previous = start_block
    current = (apply_operator(start_block, edge_weights, scaling) - centre * start_block) / spread
    for order_now in range(1, DEGREE):
        following = (
            2.0 * (apply_operator(current, edge_weights, scaling) - centre * current) / spread
            - previous
        )
        previous, current = (current, following)
    return current


def block_gram(flat_block):
    return jnp.dot(
        flat_block,
        flat_block.T,
        precision=lax.Precision.HIGHEST,
        preferred_element_type=jnp.float32,
    )


def on_device(start_block, edge_weights, mass, locked):
    scaling = 1.0 / jnp.sqrt(mass)
    filtered = chebyshev(start_block, edge_weights, scaling)
    block_count = filtered.shape[0]
    vertices = (
        filtered.shape[1]
        * filtered.shape[2]
        * lax.axis_size(("strip", "sub"))
        * lax.axis_size("panel")
    )
    identity_matrix = jnp.eye(block_count, dtype=jnp.float32)
    whole_rows = lax.all_gather(filtered, "panel", axis=2, tiled=True)
    flat_whole = whole_rows.reshape(block_count, -1)
    gram_matrix = (
        lax.psum(block_gram(flat_whole), ("strip", "sub")) / vertices + 1e-06 * identity_matrix
    )
    lower_factor = jnp.linalg.cholesky(gram_matrix)
    ortho_whole = lax.linalg.triangular_solve(
        lower_factor, flat_whole, left_side=True, lower=True
    ).reshape(whole_rows.shape)
    own_width = filtered.shape[2]
    ortho = lax.dynamic_slice_in_dim(ortho_whole, lax.axis_index("panel") * own_width, own_width, 2)
    ortho_half = ortho_whole.astype(jnp.bfloat16).reshape(block_count, -1)
    locked_flat = locked.reshape(locked.shape[0], -1)
    partial_coupling = jnp.einsum(
        "kn,bn->kb", locked_flat, ortho_half, preferred_element_type=jnp.float32
    )
    coupling = lax.psum(partial_coupling, ("strip", "sub")) / math.sqrt(float(vertices))
    return (ortho, coupling, jnp.transpose(lower_factor))


def solution(mesh):
    return jax.shard_map(
        on_device,
        mesh=mesh,
        in_specs=(
            P("groups", ("strip", "sub"), "panel"),
            P("groups", ("strip", "sub"), "panel"),
            P(("groups", "strip", "sub"), "panel"),
            P(("groups", "panel"), ("strip", "sub"), None),
        ),
        out_specs=(
            P("groups", ("strip", "sub"), "panel"),
            P(("groups", "panel"), None),
            P("groups", None),
        ),
        check_vma=False,
    )
```

profile of v0, /device:TPU:0, one launch (start us, length us, event | category | flops | bytes accessed | tf_op | source)
XLA Modules:
  0.0 241.3 jit_solution(13510634319213485302)
XLA Ops:
  12.7 4.0 %collective-permute-done.1 = f32[32,1,128]{2,0,1:T(8,128)S(1)} collective-permute-done((f32[32,1,128]{2,0,1:T(8,128)S(1)}, f32[32,1,128]{2,0,1:T(8,128)S(1)}, u32[]{:S(2)}, u32[]{:S(2)}) %collective-permute-start.1) | collective-permute-done | bytes 16416 | tf_op jit(solution)/shard_map/ppermute | solution.py:21
  18.1 4.6 %collective-permute-start.3 = (f32[32,18,1]{2,0,1:T(8,128)S(1)}, f32[32,18,1]{2,0,1:T(8,128)S(1)}, u32[]{:S(2)}, u32[]{:S(2)}) collective-permute-start(f32[32,18,1]{2,0,1:T(8,128)S(1)} %get-tuple-element.41), channel_id=1, source_target_pairs={{0,2},{1,3},{4,6},{5,7},{8,10},{9,11},{12,14},{13,15},{16,18},{17,... | collective-permute-start | bytes 6920 | tf_op jit(solution)/shard_map/ppermute | solution.py:20
  23.5 3.5 %collective-permute-done.2 = f32[32,18,1]{2,0,1:T(8,128)S(1)} collective-permute-done((f32[32,18,1]{2,0,1:T(8,128)S(1)}, f32[32,18,1]{2,0,1:T(8,128)S(1)}, u32[]{:S(2)}, u32[]{:S(2)}) %collective-permute-start.2) | collective-permute-done | bytes 2336 | tf_op jit(solution)/shard_map/ppermute | solution.py:21
  29.5 3.3 %collective-permute-start.4 = (f32[32,1,128]{2,0,1:T(8,128)S(1)}, f32[32,1,128]{2,0,1:T(8,128)S(1)}, u32[]{:S(2)}, u32[]{:S(2)}) collective-permute-start(f32[32,1,128]{2,0,1:T(8,128)S(1)} %get-tuple-element.51), channel_id=1, source_target_pairs={{0,1},{1,4},{4,5},{5,8},{8,9},{9,12},{12,13},{2,3},{3,6},{6,7},{7,... | collective-permute-start | bytes 49160 | tf_op jit(solution)/shard_map/ppermute | solution.py:20
  34.1 3.3 %collective-permute-done.5 = f32[32,1,128]{2,0,1:T(8,128)S(1)} collective-permute-done((f32[32,1,128]{2,0,1:T(8,128)S(1)}, f32[32,1,128]{2,0,1:T(8,128)S(1)}, u32[]{:S(2)}, u32[]{:S(2)}) %collective-permute-start.5) | collective-permute-done | bytes 16416 | tf_op jit(solution)/shard_map/ppermute | solution.py:21
  38.9 4.6 %collective-permute-start.7 = (f32[32,18,1]{2,0,1:T(8,128)S(1)}, f32[32,18,1]{2,0,1:T(8,128)S(1)}, u32[]{:S(2)}, u32[]{:S(2)}) collective-permute-start(f32[32,18,1]{2,0,1:T(8,128)S(1)} %get-tuple-element.37), channel_id=1, source_target_pairs={{0,2},{1,3},{4,6},{5,7},{8,10},{9,11},{12,14},{13,15},{16,18},{17,... | collective-permute-start | bytes 6920 | tf_op jit(solution)/shard_map/ppermute | solution.py:20
  43.5 4.2 %collective-permute-done.6 = f32[32,18,1]{2,0,1:T(8,128)S(1)} collective-permute-done((f32[32,18,1]{2,0,1:T(8,128)S(1)}, f32[32,18,1]{2,0,1:T(8,128)S(1)}, u32[]{:S(2)}, u32[]{:S(2)}) %collective-permute-start.6) | collective-permute-done | bytes 2336 | tf_op jit(solution)/shard_map/ppermute | solution.py:21
  50.2 3.4 %collective-permute-start.8 = (f32[32,1,128]{2,0,1:T(8,128)S(1)}, f32[32,1,128]{2,0,1:T(8,128)S(1)}, u32[]{:S(2)}, u32[]{:S(2)}) collective-permute-start(f32[32,1,128]{2,0,1:T(8,128)S(1)} %get-tuple-element.49), channel_id=1, source_target_pairs={{0,1},{1,4},{4,5},{5,8},{8,9},{9,12},{12,13},{2,3},{3,6},{6,7},{7,... | collective-permute-start | bytes 49160 | tf_op jit(solution)/shard_map/ppermute | solution.py:20
  59.6 4.6 %collective-permute-start.11 = (f32[32,18,1]{2,0,1:T(8,128)S(1)}, f32[32,18,1]{2,0,1:T(8,128)S(1)}, u32[]{:S(2)}, u32[]{:S(2)}) collective-permute-start(f32[32,18,1]{2,0,1:T(8,128)S(1)} %get-tuple-element.33), channel_id=1, source_target_pairs={{0,2},{1,3},{4,6},{5,7},{8,10},{9,11},{12,14},{13,15},{16,18},{17,... | collective-permute-start | bytes 6920 | tf_op jit(solution)/shard_map/ppermute | solution.py:20
  64.2 4.2 %collective-permute-done.10 = f32[32,18,1]{2,0,1:T(8,128)S(1)} collective-permute-done((f32[32,18,1]{2,0,1:T(8,128)S(1)}, f32[32,18,1]{2,0,1:T(8,128)S(1)}, u32[]{:S(2)}, u32[]{:S(2)}) %collective-permute-start.10) | collective-permute-done | bytes 2336 | tf_op jit(solution)/shard_map/ppermute | solution.py:21
  70.8 3.4 %collective-permute-start.12 = (f32[32,1,128]{2,0,1:T(8,128)S(1)}, f32[32,1,128]{2,0,1:T(8,128)S(1)}, u32[]{:S(2)}, u32[]{:S(2)}) collective-permute-start(f32[32,1,128]{2,0,1:T(8,128)S(1)} %get-tuple-element.47), channel_id=1, source_target_pairs={{0,1},{1,4},{4,5},{5,8},{8,9},{9,12},{12,13},{2,3},{3,6},{6,7},{7,... | collective-permute-start | bytes 49160 | tf_op jit(solution)/shard_map/ppermute | solution.py:20
  75.6 3.5 %collective-permute-done.13 = f32[32,1,128]{2,0,1:T(8,128)S(1)} collective-permute-done((f32[32,1,128]{2,0,1:T(8,128)S(1)}, f32[32,1,128]{2,0,1:T(8,128)S(1)}, u32[]{:S(2)}, u32[]{:S(2)}) %collective-permute-start.13) | collective-permute-done | bytes 16416 | tf_op jit(solution)/shard_map/ppermute | solution.py:21
  80.5 4.6 %collective-permute-start.15 = (f32[32,18,1]{2,0,1:T(8,128)S(1)}, f32[32,18,1]{2,0,1:T(8,128)S(1)}, u32[]{:S(2)}, u32[]{:S(2)}) collective-permute-start(f32[32,18,1]{2,0,1:T(8,128)S(1)} %get-tuple-element.29), channel_id=1, source_target_pairs={{0,2},{1,3},{4,6},{5,7},{8,10},{9,11},{12,14},{13,15},{16,18},{17,... | collective-permute-start | bytes 6920 | tf_op jit(solution)/shard_map/ppermute | solution.py:20
  85.1 4.2 %collective-permute-done.14 = f32[32,18,1]{2,0,1:T(8,128)S(1)} collective-permute-done((f32[32,18,1]{2,0,1:T(8,128)S(1)}, f32[32,18,1]{2,0,1:T(8,128)S(1)}, u32[]{:S(2)}, u32[]{:S(2)}) %collective-permute-start.14) | collective-permute-done | bytes 2336 | tf_op jit(solution)/shard_map/ppermute | solution.py:21
  91.8 3.4 %collective-permute-start.16 = (f32[32,1,128]{2,0,1:T(8,128)S(1)}, f32[32,1,128]{2,0,1:T(8,128)S(1)}, u32[]{:S(2)}, u32[]{:S(2)}) collective-permute-start(f32[32,1,128]{2,0,1:T(8,128)S(1)} %get-tuple-element.45), channel_id=1, source_target_pairs={{0,1},{1,4},{4,5},{5,8},{8,9},{9,12},{12,13},{2,3},{3,6},{6,7},{7,... | collective-permute-start | bytes 49160 | tf_op jit(solution)/shard_map/ppermute | solution.py:20
  100.7 4.6 %collective-permute-start.19 = (f32[32,18,1]{2,0,1:T(8,128)S(1)}, f32[32,18,1]{2,0,1:T(8,128)S(1)}, u32[]{:S(2)}, u32[]{:S(2)}) collective-permute-start(f32[32,18,1]{2,0,1:T(8,128)S(1)} %get-tuple-element.25), channel_id=1, source_target_pairs={{0,2},{1,3},{4,6},{5,7},{8,10},{9,11},{12,14},{13,15},{16,18},{17,... | collective-permute-start | bytes 6920 | tf_op jit(solution)/shard_map/ppermute | solution.py:20
  105.3 4.2 %collective-permute-done.18 = f32[32,18,1]{2,0,1:T(8,128)S(1)} collective-permute-done((f32[32,18,1]{2,0,1:T(8,128)S(1)}, f32[32,18,1]{2,0,1:T(8,128)S(1)}, u32[]{:S(2)}, u32[]{:S(2)}) %collective-permute-start.18) | collective-permute-done | bytes 2336 | tf_op jit(solution)/shard_map/ppermute | solution.py:21
  111.9 3.4 %collective-permute-start.20 = (f32[32,1,128]{2,0,1:T(8,128)S(1)}, f32[32,1,128]{2,0,1:T(8,128)S(1)}, u32[]{:S(2)}, u32[]{:S(2)}) collective-permute-start(f32[32,1,128]{2,0,1:T(8,128)S(1)} %get-tuple-element.43), channel_id=1, source_target_pairs={{0,1},{1,4},{4,5},{5,8},{8,9},{9,12},{12,13},{2,3},{3,6},{6,7},{7,... | collective-permute-start | bytes 49160 | tf_op jit(solution)/shard_map/ppermute | solution.py:20
  119.9 4.6 %collective-permute-start.23 = (f32[32,18,1]{2,0,1:T(8,128)S(1)}, f32[32,18,1]{2,0,1:T(8,128)S(1)}, u32[]{:S(2)}, u32[]{:S(2)}) collective-permute-start(f32[32,18,1]{2,0,1:T(8,128)S(1)} %get-tuple-element.21), channel_id=1, source_target_pairs={{0,2},{1,3},{4,6},{5,7},{8,10},{9,11},{12,14},{13,15},{16,18},{17,... | collective-permute-start | bytes 6920 | tf_op jit(solution)/shard_map/ppermute | solution.py:20
  124.5 4.3 %collective-permute-done.22 = f32[32,18,1]{2,0,1:T(8,128)S(1)} collective-permute-done((f32[32,18,1]{2,0,1:T(8,128)S(1)}, f32[32,18,1]{2,0,1:T(8,128)S(1)}, u32[]{:S(2)}, u32[]{:S(2)}) %collective-permute-start.22) | collective-permute-done | bytes 2336 | tf_op jit(solution)/shard_map/ppermute | solution.py:21
  131.2 9.9 %all_gather.3 = f32[32,16,256]{2,0,1:T(8,128)S(1)} all-gather(f32[32,16,128]{2,0,1:T(8,128)S(1)} %fusion.13), channel_id=1, replica_groups=mesh['groups'=2,'strip'=4,'panel'=2,'sub'=2] {'panel'}, dimensions={2}, use_global_device_ids=true | all-gather | bytes 786432 | tf_op jit(solution)/shard_map/all_gather | solution.py:75
  141.7 26.0 %psum.14 = f32[32,32]{1,0:T(8,128)S(1)} all-reduce(f32[32,32]{1,0:T(8,128)S(1)} %convolution_bitcast_fusion), channel_id=1, replica_groups=mesh['groups'=2,'strip'=4,'panel'=2,'sub'=2] {'strip','sub'}, use_global_device_ids=true, to_apply=%region_0.0 | all-reduce | flops 1024 | bytes 8192 | tf_op jit(solution)/shard_map/psum | solution.py:78
  175.2 5.2 %fusion.2 = f32[512,32]{0,1:T(8,128)} fusion(bf16[512,16,256]{2,1,0:T(8,128)(2,1)} %param.7, f32[32,16,256]{2,0,1:T(8,128)S(1)} %fusion.5), kind=kOutput, calls=%fused_computation.2 | convolution fusion | flops 134348800 | bytes 4784128 | tf_op jit(solution)/shard_map/kn,bn->kb/dot_general | solution.py:88
  181.9 51.1 %all-reduce.2.cloned.1.call-done = f32[512,32]{0,1:T(8,128)} async-done(((f32[512,32]{0,1:T(8,128)}), f32[512,32]{0,1:T(8,128)}) %all-reduce.2.cloned.1.call-update) | async-done | bytes 65552 | tf_op jit(solution)/shard_map/psum | solution.py:91
  (79 shorter events, 55.0 us)
Async XLA Ops:
  7.2 225.8 %all-reduce.2.cloned.1.call-start = ((), (), s32[]{:S(2)}) async-start(), calls=%async_computation | async-start | bytes 131072 | tf_op jit(solution)/shard_map/psum | solution.py:91
  9.0 3.7 %collective-permute-start = (f32[32,1,128]{2,0,1:T(8,128)S(1)}, f32[32,1,128]{2,0,1:T(8,128)S(1)}, u32[]{:S(2)}, u32[]{:S(2)}) collective-permute-start(f32[32,1,128]{2,0,1:T(8,128)S(1)} %get-tuple-element.53), channel_id=1, source_target_pairs={{0,1},{1,4},{4,5},{5,8},{8,9},{9,12},{12,13},{2,3},{3,6},{6,7},{7,... | collective-permute-start | bytes 49160 | tf_op jit(solution)/shard_map/ppermute | solution.py:20
  11.4 5.3 %collective-permute-start.1 = (f32[32,1,128]{2,0,1:T(8,128)S(1)}, f32[32,1,128]{2,0,1:T(8,128)S(1)}, u32[]{:S(2)}, u32[]{:S(2)}) collective-permute-start(f32[32,1,128]{2,0,1:T(8,128)S(1)} %get-tuple-element.54), channel_id=1, source_target_pairs={{1,0},{4,1},{5,4},{8,5},{9,8},{12,9},{13,12},{3,2},{6,3},{7,6},{10... | collective-permute-start | bytes 49160 | tf_op jit(solution)/shard_map/ppermute | solution.py:21
  16.8 10.2 %collective-permute-start.2 = (f32[32,18,1]{2,0,1:T(8,128)S(1)}, f32[32,18,1]{2,0,1:T(8,128)S(1)}, u32[]{:S(2)}, u32[]{:S(2)}) collective-permute-start(f32[32,18,1]{2,0,1:T(8,128)S(1)} %get-tuple-element.42), channel_id=1, source_target_pairs={{2,0},{3,1},{6,4},{7,5},{10,8},{11,9},{14,12},{15,13},{18,16},{19,... | collective-permute-start | bytes 6920 | tf_op jit(solution)/shard_map/ppermute | solution.py:21
  18.1 10.7 %collective-permute-start.3 = (f32[32,18,1]{2,0,1:T(8,128)S(1)}, f32[32,18,1]{2,0,1:T(8,128)S(1)}, u32[]{:S(2)}, u32[]{:S(2)}) collective-permute-start(f32[32,18,1]{2,0,1:T(8,128)S(1)} %get-tuple-element.41), channel_id=1, source_target_pairs={{0,2},{1,3},{4,6},{5,7},{8,10},{9,11},{12,14},{13,15},{16,18},{17,... | collective-permute-start | bytes 6920 | tf_op jit(solution)/shard_map/ppermute | solution.py:20
  29.5 4.6 %collective-permute-start.4 = (f32[32,1,128]{2,0,1:T(8,128)S(1)}, f32[32,1,128]{2,0,1:T(8,128)S(1)}, u32[]{:S(2)}, u32[]{:S(2)}) collective-permute-start(f32[32,1,128]{2,0,1:T(8,128)S(1)} %get-tuple-element.51), channel_id=1, source_target_pairs={{0,1},{1,4},{4,5},{5,8},{8,9},{9,12},{12,13},{2,3},{3,6},{6,7},{7,... | collective-permute-start | bytes 49160 | tf_op jit(solution)/shard_map/ppermute | solution.py:20
  32.8 4.6 %collective-permute-start.5 = (f32[32,1,128]{2,0,1:T(8,128)S(1)}, f32[32,1,128]{2,0,1:T(8,128)S(1)}, u32[]{:S(2)}, u32[]{:S(2)}) collective-permute-start(f32[32,1,128]{2,0,1:T(8,128)S(1)} %get-tuple-element.52), channel_id=1, source_target_pairs={{1,0},{4,1},{5,4},{8,5},{9,8},{12,9},{13,12},{3,2},{6,3},{7,6},{10... | collective-permute-start | bytes 49160 | tf_op jit(solution)/shard_map/ppermute | solution.py:21
  37.6 10.1 %collective-permute-start.6 = (f32[32,18,1]{2,0,1:T(8,128)S(1)}, f32[32,18,1]{2,0,1:T(8,128)S(1)}, u32[]{:S(2)}, u32[]{:S(2)}) collective-permute-start(f32[32,18,1]{2,0,1:T(8,128)S(1)} %get-tuple-element.38), channel_id=1, source_target_pairs={{2,0},{3,1},{6,4},{7,5},{10,8},{11,9},{14,12},{15,13},{18,16},{19,... | collective-permute-start | bytes 6920 | tf_op jit(solution)/shard_map/ppermute | solution.py:21
  38.9 10.6 %collective-permute-start.7 = (f32[32,18,1]{2,0,1:T(8,128)S(1)}, f32[32,18,1]{2,0,1:T(8,128)S(1)}, u32[]{:S(2)}, u32[]{:S(2)}) collective-permute-start(f32[32,18,1]{2,0,1:T(8,128)S(1)} %get-tuple-element.37), channel_id=1, source_target_pairs={{0,2},{1,3},{4,6},{5,7},{8,10},{9,11},{12,14},{13,15},{16,18},{17,... | collective-permute-start | bytes 6920 | tf_op jit(solution)/shard_map/ppermute | solution.py:20
  50.2 4.7 %collective-permute-start.8 = (f32[32,1,128]{2,0,1:T(8,128)S(1)}, f32[32,1,128]{2,0,1:T(8,128)S(1)}, u32[]{:S(2)}, u32[]{:S(2)}) collective-permute-start(f32[32,1,128]{2,0,1:T(8,128)S(1)} %get-tuple-element.49), channel_id=1, source_target_pairs={{0,1},{1,4},{4,5},{5,8},{8,9},{9,12},{12,13},{2,3},{3,6},{6,7},{7,... | collective-permute-start | bytes 49160 | tf_op jit(solution)/shard_map/ppermute | solution.py:20
  53.6 4.5 %collective-permute-start.9 = (f32[32,1,128]{2,0,1:T(8,128)S(1)}, f32[32,1,128]{2,0,1:T(8,128)S(1)}, u32[]{:S(2)}, u32[]{:S(2)}) collective-permute-start(f32[32,1,128]{2,0,1:T(8,128)S(1)} %get-tuple-element.50), channel_id=1, source_target_pairs={{1,0},{4,1},{5,4},{8,5},{9,8},{12,9},{13,12},{3,2},{6,3},{7,6},{10... | collective-permute-start | bytes 49160 | tf_op jit(solution)/shard_map/ppermute | solution.py:21
  58.3 10.1 %collective-permute-start.10 = (f32[32,18,1]{2,0,1:T(8,128)S(1)}, f32[32,18,1]{2,0,1:T(8,128)S(1)}, u32[]{:S(2)}, u32[]{:S(2)}) collective-permute-start(f32[32,18,1]{2,0,1:T(8,128)S(1)} %get-tuple-element.34), channel_id=1, source_target_pairs={{2,0},{3,1},{6,4},{7,5},{10,8},{11,9},{14,12},{15,13},{18,16},{19,... | collective-permute-start | bytes 6920 | tf_op jit(solution)/shard_map/ppermute | solution.py:21
  59.6 10.6 %collective-permute-start.11 = (f32[32,18,1]{2,0,1:T(8,128)S(1)}, f32[32,18,1]{2,0,1:T(8,128)S(1)}, u32[]{:S(2)}, u32[]{:S(2)}) collective-permute-start(f32[32,18,1]{2,0,1:T(8,128)S(1)} %get-tuple-element.33), channel_id=1, source_target_pairs={{0,2},{1,3},{4,6},{5,7},{8,10},{9,11},{12,14},{13,15},{16,18},{17,... | collective-permute-start | bytes 6920 | tf_op jit(solution)/shard_map/ppermute | solution.py:20
  70.8 4.7 %collective-permute-start.12 = (f32[32,1,128]{2,0,1:T(8,128)S(1)}, f32[32,1,128]{2,0,1:T(8,128)S(1)}, u32[]{:S(2)}, u32[]{:S(2)}) collective-permute-start(f32[32,1,128]{2,0,1:T(8,128)S(1)} %get-tuple-element.47), channel_id=1, source_target_pairs={{0,1},{1,4},{4,5},{5,8},{8,9},{9,12},{12,13},{2,3},{3,6},{6,7},{7,... | collective-permute-start | bytes 49160 | tf_op jit(solution)/shard_map/ppermute | solution.py:20
  74.3 4.8 %collective-permute-start.13 = (f32[32,1,128]{2,0,1:T(8,128)S(1)}, f32[32,1,128]{2,0,1:T(8,128)S(1)}, u32[]{:S(2)}, u32[]{:S(2)}) collective-permute-start(f32[32,1,128]{2,0,1:T(8,128)S(1)} %get-tuple-element.48), channel_id=1, source_target_pairs={{1,0},{4,1},{5,4},{8,5},{9,8},{12,9},{13,12},{3,2},{6,3},{7,6},{10... | collective-permute-start | bytes 49160 | tf_op jit(solution)/shard_map/ppermute | solution.py:21
  79.2 10.1 %collective-permute-start.14 = (f32[32,18,1]{2,0,1:T(8,128)S(1)}, f32[32,18,1]{2,0,1:T(8,128)S(1)}, u32[]{:S(2)}, u32[]{:S(2)}) collective-permute-start(f32[32,18,1]{2,0,1:T(8,128)S(1)} %get-tuple-element.30), channel_id=1, source_target_pairs={{2,0},{3,1},{6,4},{7,5},{10,8},{11,9},{14,12},{15,13},{18,16},{19,... | collective-permute-start | bytes 6920 | tf_op jit(solution)/shard_map/ppermute | solution.py:21
  80.5 10.6 %collective-permute-start.15 = (f32[32,18,1]{2,0,1:T(8,128)S(1)}, f32[32,18,1]{2,0,1:T(8,128)S(1)}, u32[]{:S(2)}, u32[]{:S(2)}) collective-permute-start(f32[32,18,1]{2,0,1:T(8,128)S(1)} %get-tuple-element.29), channel_id=1, source_target_pairs={{0,2},{1,3},{4,6},{5,7},{8,10},{9,11},{12,14},{13,15},{16,18},{17,... | collective-permute-start | bytes 6920 | tf_op jit(solution)/shard_map/ppermute | solution.py:20
  91.8 4.7 %collective-permute-start.16 = (f32[32,1,128]{2,0,1:T(8,128)S(1)}, f32[32,1,128]{2,0,1:T(8,128)S(1)}, u32[]{:S(2)}, u32[]{:S(2)}) collective-permute-start(f32[32,1,128]{2,0,1:T(8,128)S(1)} %get-tuple-element.45), channel_id=1, source_target_pairs={{0,1},{1,4},{4,5},{5,8},{8,9},{9,12},{12,13},{2,3},{3,6},{6,7},{7,... | collective-permute-start | bytes 49160 | tf_op jit(solution)/shard_map/ppermute | solution.py:20
  95.2 4.0 %collective-permute-start.17 = (f32[32,1,128]{2,0,1:T(8,128)S(1)}, f32[32,1,128]{2,0,1:T(8,128)S(1)}, u32[]{:S(2)}, u32[]{:S(2)}) collective-permute-start(f32[32,1,128]{2,0,1:T(8,128)S(1)} %get-tuple-element.46), channel_id=1, source_target_pairs={{1,0},{4,1},{5,4},{8,5},{9,8},{12,9},{13,12},{3,2},{6,3},{7,6},{10... | collective-permute-start | bytes 49160 | tf_op jit(solution)/shard_map/ppermute | solution.py:21
  99.4 10.1 %collective-permute-start.18 = (f32[32,18,1]{2,0,1:T(8,128)S(1)}, f32[32,18,1]{2,0,1:T(8,128)S(1)}, u32[]{:S(2)}, u32[]{:S(2)}) collective-permute-start(f32[32,18,1]{2,0,1:T(8,128)S(1)} %get-tuple-element.26), channel_id=1, source_target_pairs={{2,0},{3,1},{6,4},{7,5},{10,8},{11,9},{14,12},{15,13},{18,16},{19,... | collective-permute-start | bytes 6920 | tf_op jit(solution)/shard_map/ppermute | solution.py:21
  100.7 10.6 %collective-permute-start.19 = (f32[32,18,1]{2,0,1:T(8,128)S(1)}, f32[32,18,1]{2,0,1:T(8,128)S(1)}, u32[]{:S(2)}, u32[]{:S(2)}) collective-permute-start(f32[32,18,1]{2,0,1:T(8,128)S(1)} %get-tuple-element.25), channel_id=1, source_target_pairs={{0,2},{1,3},{4,6},{5,7},{8,10},{9,11},{12,14},{13,15},{16,18},{17,... | collective-permute-start | bytes 6920 | tf_op jit(solution)/shard_map/ppermute | solution.py:20
  111.9 4.7 %collective-permute-start.20 = (f32[32,1,128]{2,0,1:T(8,128)S(1)}, f32[32,1,128]{2,0,1:T(8,128)S(1)}, u32[]{:S(2)}, u32[]{:S(2)}) collective-permute-start(f32[32,1,128]{2,0,1:T(8,128)S(1)} %get-tuple-element.43), channel_id=1, source_target_pairs={{0,1},{1,4},{4,5},{5,8},{8,9},{9,12},{12,13},{2,3},{3,6},{6,7},{7,... | collective-permute-start | bytes 49160 | tf_op jit(solution)/shard_map/ppermute | solution.py:20
  118.6 10.1 %collective-permute-start.22 = (f32[32,18,1]{2,0,1:T(8,128)S(1)}, f32[32,18,1]{2,0,1:T(8,128)S(1)}, u32[]{:S(2)}, u32[]{:S(2)}) collective-permute-start(f32[32,18,1]{2,0,1:T(8,128)S(1)} %get-tuple-element.22), channel_id=1, source_target_pairs={{2,0},{3,1},{6,4},{7,5},{10,8},{11,9},{14,12},{15,13},{18,16},{19,... | collective-permute-start | bytes 6920 | tf_op jit(solution)/shard_map/ppermute | solution.py:21
  119.9 10.6 %collective-permute-start.23 = (f32[32,18,1]{2,0,1:T(8,128)S(1)}, f32[32,18,1]{2,0,1:T(8,128)S(1)}, u32[]{:S(2)}, u32[]{:S(2)}) collective-permute-start(f32[32,18,1]{2,0,1:T(8,128)S(1)} %get-tuple-element.21), channel_id=1, source_target_pairs={{0,2},{1,3},{4,6},{5,7},{8,10},{9,11},{12,14},{13,15},{16,18},{17,... | collective-permute-start | bytes 6920 | tf_op jit(solution)/shard_map/ppermute | solution.py:20
  (2 other events, 25.0 us)
Sparse Core Ops, SparseCore 0:
  180.5 52.4 all-reduce.1
where the time goes:
time: 242 us; the launch traced here: 241 us
  waiting for transfers between devices  105 us (43%)
  starting transfers between devices  62.3 us (26%)
  blocking collectives  35.9 us (15%)
  between operations  14.5 us (6%)
  other arithmetic  14.2 us (6%)
  matrix products  6.4 us (3%)
  local copies, waits for them, and re-layouts  3.36 us (1%)
    psum x1, waiting for transfers between devices, on_device(): lax.psum(partial_coupling, ('strip', 'sub')) / math.sqrt(float(vertices))  51.1 us
    ppermute x12, starting transfers between devices, with_halo(): before = lax.ppermute(last, axis, up)  46.8 us
    ppermute x12, waiting for transfers between devices, with_halo(): after = lax.ppermute(leading, axis, down)  42.9 us
    psum x1, blocking collectives, on_device(): lax.psum(block_gram(flat_whole), ('strip', 'sub')) / vertices  26 us
    ppermute x12, starting transfers between devices, with_halo(): after = lax.ppermute(leading, axis, down)  15.5 us
    ppermute x12, waiting for transfers between devices, with_halo(): before = lax.ppermute(last, axis, up)  10.7 us
    all_gather x1, blocking collectives, on_device(): whole_rows = lax.all_gather(filtered, 'panel', axis=2, tiled=True)  9.93 us
    dot_general x1, matrix products, on_device(): jnp.einsum('kn,bn->kb', locked_flat, ortho_half, preferred_element_type=j...  5.19 us
  transfers between devices with their start and end apart: 25, of which 19 were waited for; matrix products, arithmetic and copies ran while one was open for 1% of the time, Pallas kernels for 0%

commit v1 on v0

--- a/solution.py
+++ b/solution.py
@@ -88,7 +88,9 @@
     partial_coupling = jnp.einsum(
         "kn,bn->kb", locked_flat, ortho_half, preferred_element_type=jnp.float32
     )
-    coupling = lax.psum(partial_coupling, ("strip", "sub")) / math.sqrt(float(vertices))
+    coupling = jnp.sum(jax.lax.all_gather(partial_coupling, ("strip", "sub")), axis=0) / math.sqrt(
+        float(vertices)
+    )
     return (ortho, coupling, jnp.transpose(lower_factor))
 
 

time: 242 us -> 192 us (0.79)
  waiting for transfers between devices: 105 us -> 53.6 us
  blocking collectives: 35.9 us -> 50.9 us
  between operations: 14.5 us -> 1.11 us
    psum x1 -> x0, waiting for transfers between devices: 51.1 us -> none  [on_device(): lax.psum(partial_coupling, ('strip', 'sub')) / math.sqrt(float(vertices))]
    all_gather x0 -> x1, blocking collectives: none -> 15 us  [on_device(): jax.lax.all_gather(partial_coupling, ('strip', 'sub'))]
  transfers between devices with their start and end apart: 25 -> 24, of which waited for: 19 -> 18; matrix products, arithmetic and copies ran while one was open for 1% -> 0% of each run, Pallas kernels for 0% -> 0%
where the time goes in v1:
time: 192 us; the launch traced here: 191 us
  starting transfers between devices  62.3 us (32%)
  waiting for transfers between devices  53.6 us (28%)
  blocking collectives  50.9 us (27%)
  other arithmetic  13.4 us (7%)
  matrix products  5.77 us (3%)
  local copies, waits for them, and re-layouts  3.66 us (2%)
    ppermute x12, starting transfers between devices, with_halo(): before = lax.ppermute(last, axis, up)  46.8 us
    ppermute x12, waiting for transfers between devices, with_halo(): after = lax.ppermute(leading, axis, down)  42.9 us
    psum x1, blocking collectives, on_device(): lax.psum(block_gram(flat_whole), ('strip', 'sub')) / vertices  26 us
    ppermute x12, starting transfers between devices, with_halo(): after = lax.ppermute(leading, axis, down)  15.5 us
    all_gather x1, blocking collectives, on_device(): jax.lax.all_gather(partial_coupling, ('strip', 'sub'))  15 us
    ppermute x12, waiting for transfers between devices, with_halo(): before = lax.ppermute(last, axis, up)  10.7 us
    all_gather x1, blocking collectives, on_device(): whole_rows = lax.all_gather(filtered, 'panel', axis=2, tiled=True)  9.93 us
    dot_general x1, matrix products, on_device(): jnp.einsum('kn,bn->kb', locked_flat, ortho_half, preferred_element_type=j...  4.57 us
  transfers between devices with their start and end apart: 24, of which 18 were waited for; matrix products, arithmetic and copies ran while one was open for 0% of the time, Pallas kernels for 0%

profile of v1, /device:TPU:0, one launch (start us, length us, event | category | flops | bytes accessed | tf_op | source)
XLA Modules:
  0.0 190.7 jit_solution(10894134431964838497)
XLA Ops:
  6.1 4.0 %collective-permute-done.1 = f32[32,1,128]{2,0,1:T(8,128)S(1)} collective-permute-done((f32[32,1,128]{2,0,1:T(8,128)S(1)}, f32[32,1,128]{2,0,1:T(8,128)S(1)}, u32[]{:S(2)}, u32[]{:S(2)}) %collective-permute-start.1) | collective-permute-done | bytes 16416 | tf_op jit(solution)/shard_map/ppermute | solution.py:21
  11.6 4.6 %collective-permute-start.3 = (f32[32,18,1]{2,0,1:T(8,128)S(1)}, f32[32,18,1]{2,0,1:T(8,128)S(1)}, u32[]{:S(2)}, u32[]{:S(2)}) collective-permute-start(f32[32,18,1]{2,0,1:T(8,128)S(1)} %get-tuple-element.41), channel_id=1, source_target_pairs={{0,2},{1,3},{4,6},{5,7},{8,10},{9,11},{12,14},{13,15},{16,18},{17,... | collective-permute-start | bytes 6920 | tf_op jit(solution)/shard_map/ppermute | solution.py:20
  17.0 3.5 %collective-permute-done.2 = f32[32,18,1]{2,0,1:T(8,128)S(1)} collective-permute-done((f32[32,18,1]{2,0,1:T(8,128)S(1)}, f32[32,18,1]{2,0,1:T(8,128)S(1)}, u32[]{:S(2)}, u32[]{:S(2)}) %collective-permute-start.2) | collective-permute-done | bytes 2336 | tf_op jit(solution)/shard_map/ppermute | solution.py:21
  22.9 3.3 %collective-permute-start.4 = (f32[32,1,128]{2,0,1:T(8,128)S(1)}, f32[32,1,128]{2,0,1:T(8,128)S(1)}, u32[]{:S(2)}, u32[]{:S(2)}) collective-permute-start(f32[32,1,128]{2,0,1:T(8,128)S(1)} %get-tuple-element.51), channel_id=1, source_target_pairs={{0,1},{1,4},{4,5},{5,8},{8,9},{9,12},{12,13},{2,3},{3,6},{6,7},{7,... | collective-permute-start | bytes 49160 | tf_op jit(solution)/shard_map/ppermute | solution.py:20
  27.5 3.3 %collective-permute-done.5 = f32[32,1,128]{2,0,1:T(8,128)S(1)} collective-permute-done((f32[32,1,128]{2,0,1:T(8,128)S(1)}, f32[32,1,128]{2,0,1:T(8,128)S(1)}, u32[]{:S(2)}, u32[]{:S(2)}) %collective-permute-start.5) | collective-permute-done | bytes 16416 | tf_op jit(solution)/shard_map/ppermute | solution.py:21
  32.3 4.6 %collective-permute-start.7 = (f32[32,18,1]{2,0,1:T(8,128)S(1)}, f32[32,18,1]{2,0,1:T(8,128)S(1)}, u32[]{:S(2)}, u32[]{:S(2)}) collective-permute-start(f32[32,18,1]{2,0,1:T(8,128)S(1)} %get-tuple-element.37), channel_id=1, source_target_pairs={{0,2},{1,3},{4,6},{5,7},{8,10},{9,11},{12,14},{13,15},{16,18},{17,... | collective-permute-start | bytes 6920 | tf_op jit(solution)/shard_map/ppermute | solution.py:20
  36.9 4.2 %collective-permute-done.6 = f32[32,18,1]{2,0,1:T(8,128)S(1)} collective-permute-done((f32[32,18,1]{2,0,1:T(8,128)S(1)}, f32[32,18,1]{2,0,1:T(8,128)S(1)}, u32[]{:S(2)}, u32[]{:S(2)}) %collective-permute-start.6) | collective-permute-done | bytes 2336 | tf_op jit(solution)/shard_map/ppermute | solution.py:21
  43.6 3.4 %collective-permute-start.8 = (f32[32,1,128]{2,0,1:T(8,128)S(1)}, f32[32,1,128]{2,0,1:T(8,128)S(1)}, u32[]{:S(2)}, u32[]{:S(2)}) collective-permute-start(f32[32,1,128]{2,0,1:T(8,128)S(1)} %get-tuple-element.49), channel_id=1, source_target_pairs={{0,1},{1,4},{4,5},{5,8},{8,9},{9,12},{12,13},{2,3},{3,6},{6,7},{7,... | collective-permute-start | bytes 49160 | tf_op jit(solution)/shard_map/ppermute | solution.py:20
  53.0 4.6 %collective-permute-start.11 = (f32[32,18,1]{2,0,1:T(8,128)S(1)}, f32[32,18,1]{2,0,1:T(8,128)S(1)}, u32[]{:S(2)}, u32[]{:S(2)}) collective-permute-start(f32[32,18,1]{2,0,1:T(8,128)S(1)} %get-tuple-element.33), channel_id=1, source_target_pairs={{0,2},{1,3},{4,6},{5,7},{8,10},{9,11},{12,14},{13,15},{16,18},{17,... | collective-permute-start | bytes 6920 | tf_op jit(solution)/shard_map/ppermute | solution.py:20
  57.6 4.2 %collective-permute-done.10 = f32[32,18,1]{2,0,1:T(8,128)S(1)} collective-permute-done((f32[32,18,1]{2,0,1:T(8,128)S(1)}, f32[32,18,1]{2,0,1:T(8,128)S(1)}, u32[]{:S(2)}, u32[]{:S(2)}) %collective-permute-start.10) | collective-permute-done | bytes 2336 | tf_op jit(solution)/shard_map/ppermute | solution.py:21
  64.2 3.4 %collective-permute-start.12 = (f32[32,1,128]{2,0,1:T(8,128)S(1)}, f32[32,1,128]{2,0,1:T(8,128)S(1)}, u32[]{:S(2)}, u32[]{:S(2)}) collective-permute-start(f32[32,1,128]{2,0,1:T(8,128)S(1)} %get-tuple-element.47), channel_id=1, source_target_pairs={{0,1},{1,4},{4,5},{5,8},{8,9},{9,12},{12,13},{2,3},{3,6},{6,7},{7,... | collective-permute-start | bytes 49160 | tf_op jit(solution)/shard_map/ppermute | solution.py:20
  69.0 3.5 %collective-permute-done.13 = f32[32,1,128]{2,0,1:T(8,128)S(1)} collective-permute-done((f32[32,1,128]{2,0,1:T(8,128)S(1)}, f32[32,1,128]{2,0,1:T(8,128)S(1)}, u32[]{:S(2)}, u32[]{:S(2)}) %collective-permute-start.13) | collective-permute-done | bytes 16416 | tf_op jit(solution)/shard_map/ppermute | solution.py:21
  73.9 4.6 %collective-permute-start.15 = (f32[32,18,1]{2,0,1:T(8,128)S(1)}, f32[32,18,1]{2,0,1:T(8,128)S(1)}, u32[]{:S(2)}, u32[]{:S(2)}) collective-permute-start(f32[32,18,1]{2,0,1:T(8,128)S(1)} %get-tuple-element.29), channel_id=1, source_target_pairs={{0,2},{1,3},{4,6},{5,7},{8,10},{9,11},{12,14},{13,15},{16,18},{17,... | collective-permute-start | bytes 6920 | tf_op jit(solution)/shard_map/ppermute | solution.py:20
  78.5 4.2 %collective-permute-done.14 = f32[32,18,1]{2,0,1:T(8,128)S(1)} collective-permute-done((f32[32,18,1]{2,0,1:T(8,128)S(1)}, f32[32,18,1]{2,0,1:T(8,128)S(1)}, u32[]{:S(2)}, u32[]{:S(2)}) %collective-permute-start.14) | collective-permute-done | bytes 2336 | tf_op jit(solution)/shard_map/ppermute | solution.py:21
  85.1 3.4 %collective-permute-start.16 = (f32[32,1,128]{2,0,1:T(8,128)S(1)}, f32[32,1,128]{2,0,1:T(8,128)S(1)}, u32[]{:S(2)}, u32[]{:S(2)}) collective-permute-start(f32[32,1,128]{2,0,1:T(8,128)S(1)} %get-tuple-element.45), channel_id=1, source_target_pairs={{0,1},{1,4},{4,5},{5,8},{8,9},{9,12},{12,13},{2,3},{3,6},{6,7},{7,... | collective-permute-start | bytes 49160 | tf_op jit(solution)/shard_map/ppermute | solution.py:20
  94.1 4.6 %collective-permute-start.19 = (f32[32,18,1]{2,0,1:T(8,128)S(1)}, f32[32,18,1]{2,0,1:T(8,128)S(1)}, u32[]{:S(2)}, u32[]{:S(2)}) collective-permute-start(f32[32,18,1]{2,0,1:T(8,128)S(1)} %get-tuple-element.25), channel_id=1, source_target_pairs={{0,2},{1,3},{4,6},{5,7},{8,10},{9,11},{12,14},{13,15},{16,18},{17,... | collective-permute-start | bytes 6920 | tf_op jit(solution)/shard_map/ppermute | solution.py:20
  98.7 4.2 %collective-permute-done.18 = f32[32,18,1]{2,0,1:T(8,128)S(1)} collective-permute-done((f32[32,18,1]{2,0,1:T(8,128)S(1)}, f32[32,18,1]{2,0,1:T(8,128)S(1)}, u32[]{:S(2)}, u32[]{:S(2)}) %collective-permute-start.18) | collective-permute-done | bytes 2336 | tf_op jit(solution)/shard_map/ppermute | solution.py:21
  105.3 3.4 %collective-permute-start.20 = (f32[32,1,128]{2,0,1:T(8,128)S(1)}, f32[32,1,128]{2,0,1:T(8,128)S(1)}, u32[]{:S(2)}, u32[]{:S(2)}) collective-permute-start(f32[32,1,128]{2,0,1:T(8,128)S(1)} %get-tuple-element.43), channel_id=1, source_target_pairs={{0,1},{1,4},{4,5},{5,8},{8,9},{9,12},{12,13},{2,3},{3,6},{6,7},{7,... | collective-permute-start | bytes 49160 | tf_op jit(solution)/shard_map/ppermute | solution.py:20
  113.3 4.6 %collective-permute-start.23 = (f32[32,18,1]{2,0,1:T(8,128)S(1)}, f32[32,18,1]{2,0,1:T(8,128)S(1)}, u32[]{:S(2)}, u32[]{:S(2)}) collective-permute-start(f32[32,18,1]{2,0,1:T(8,128)S(1)} %get-tuple-element.21), channel_id=1, source_target_pairs={{0,2},{1,3},{4,6},{5,7},{8,10},{9,11},{12,14},{13,15},{16,18},{17,... | collective-permute-start | bytes 6920 | tf_op jit(solution)/shard_map/ppermute | solution.py:20
  117.9 4.3 %collective-permute-done.22 = f32[32,18,1]{2,0,1:T(8,128)S(1)} collective-permute-done((f32[32,18,1]{2,0,1:T(8,128)S(1)}, f32[32,18,1]{2,0,1:T(8,128)S(1)}, u32[]{:S(2)}, u32[]{:S(2)}) %collective-permute-start.22) | collective-permute-done | bytes 2336 | tf_op jit(solution)/shard_map/ppermute | solution.py:21
  124.6 9.9 %all_gather.9 = f32[32,16,256]{2,0,1:T(8,128)S(1)} all-gather(f32[32,16,128]{2,0,1:T(8,128)S(1)} %fusion.13), channel_id=1, replica_groups=mesh['groups'=2,'strip'=4,'panel'=2,'sub'=2] {'panel'}, dimensions={2}, use_global_device_ids=true | all-gather | bytes 786432 | tf_op jit(solution)/shard_map/all_gather | solution.py:75
  135.1 26.0 %psum.7 = f32[32,32]{1,0:T(8,128)S(1)} all-reduce(f32[32,32]{1,0:T(8,128)S(1)} %convolution_bitcast_fusion), channel_id=1, replica_groups=mesh['groups'=2,'strip'=4,'panel'=2,'sub'=2] {'strip','sub'}, use_global_device_ids=true, to_apply=%region_0.0 | all-reduce | flops 1024 | bytes 8192 | tf_op jit(solution)/shard_map/psum | solution.py:78
  168.5 4.6 %fusion.2 = f32[512,32]{0,1:T(8,128)S(1)} fusion(bf16[512,16,256]{2,1,0:T(8,128)(2,1)} %param.7, f32[32,16,256]{2,0,1:T(8,128)S(1)} %fusion.5), kind=kOutput, calls=%fused_computation.2 | convolution fusion | flops 134348800 | bytes 4784128 | tf_op jit(solution)/shard_map/kn,bn->kb/dot_general | solution.py:88
  173.1 15.0 %all-gather = f32[4096,32]{0,1:T(8,128)S(1)} all-gather(f32[512,32]{0,1:T(8,128)S(1)} %fusion.2), channel_id=2, replica_groups=mesh['groups'=2,'strip'=4,'panel'=2,'sub'=2] {'strip','sub'}, dimensions={0}, use_global_device_ids=true | all-gather | bytes 589824 | tf_op jit(solution)/shard_map/all_gather | solution.py:91
  (79 shorter events, 54.5 us)
Async XLA Ops:
  2.4 3.7 %collective-permute-start = (f32[32,1,128]{2,0,1:T(8,128)S(1)}, f32[32,1,128]{2,0,1:T(8,128)S(1)}, u32[]{:S(2)}, u32[]{:S(2)}) collective-permute-start(f32[32,1,128]{2,0,1:T(8,128)S(1)} %get-tuple-element.53), channel_id=1, source_target_pairs={{0,1},{1,4},{4,5},{5,8},{8,9},{9,12},{12,13},{2,3},{3,6},{6,7},{7,... | collective-permute-start | bytes 49160 | tf_op jit(solution)/shard_map/ppermute | solution.py:20
  4.8 5.3 %collective-permute-start.1 = (f32[32,1,128]{2,0,1:T(8,128)S(1)}, f32[32,1,128]{2,0,1:T(8,128)S(1)}, u32[]{:S(2)}, u32[]{:S(2)}) collective-permute-start(f32[32,1,128]{2,0,1:T(8,128)S(1)} %get-tuple-element.54), channel_id=1, source_target_pairs={{1,0},{4,1},{5,4},{8,5},{9,8},{12,9},{13,12},{3,2},{6,3},{7,6},{10... | collective-permute-start | bytes 49160 | tf_op jit(solution)/shard_map/ppermute | solution.py:21
  10.3 10.2 %collective-permute-start.2 = (f32[32,18,1]{2,0,1:T(8,128)S(1)}, f32[32,18,1]{2,0,1:T(8,128)S(1)}, u32[]{:S(2)}, u32[]{:S(2)}) collective-permute-start(f32[32,18,1]{2,0,1:T(8,128)S(1)} %get-tuple-element.42), channel_id=1, source_target_pairs={{2,0},{3,1},{6,4},{7,5},{10,8},{11,9},{14,12},{15,13},{18,16},{19,... | collective-permute-start | bytes 6920 | tf_op jit(solution)/shard_map/ppermute | solution.py:21
  11.6 10.7 %collective-permute-start.3 = (f32[32,18,1]{2,0,1:T(8,128)S(1)}, f32[32,18,1]{2,0,1:T(8,128)S(1)}, u32[]{:S(2)}, u32[]{:S(2)}) collective-permute-start(f32[32,18,1]{2,0,1:T(8,128)S(1)} %get-tuple-element.41), channel_id=1, source_target_pairs={{0,2},{1,3},{4,6},{5,7},{8,10},{9,11},{12,14},{13,15},{16,18},{17,... | collective-permute-start | bytes 6920 | tf_op jit(solution)/shard_map/ppermute | solution.py:20
  22.9 4.6 %collective-permute-start.4 = (f32[32,1,128]{2,0,1:T(8,128)S(1)}, f32[32,1,128]{2,0,1:T(8,128)S(1)}, u32[]{:S(2)}, u32[]{:S(2)}) collective-permute-start(f32[32,1,128]{2,0,1:T(8,128)S(1)} %get-tuple-element.51), channel_id=1, source_target_pairs={{0,1},{1,4},{4,5},{5,8},{8,9},{9,12},{12,13},{2,3},{3,6},{6,7},{7,... | collective-permute-start | bytes 49160 | tf_op jit(solution)/shard_map/ppermute | solution.py:20
  26.2 4.6 %collective-permute-start.5 = (f32[32,1,128]{2,0,1:T(8,128)S(1)}, f32[32,1,128]{2,0,1:T(8,128)S(1)}, u32[]{:S(2)}, u32[]{:S(2)}) collective-permute-start(f32[32,1,128]{2,0,1:T(8,128)S(1)} %get-tuple-element.52), channel_id=1, source_target_pairs={{1,0},{4,1},{5,4},{8,5},{9,8},{12,9},{13,12},{3,2},{6,3},{7,6},{10... | collective-permute-start | bytes 49160 | tf_op jit(solution)/shard_map/ppermute | solution.py:21
  31.0 10.1 %collective-permute-start.6 = (f32[32,18,1]{2,0,1:T(8,128)S(1)}, f32[32,18,1]{2,0,1:T(8,128)S(1)}, u32[]{:S(2)}, u32[]{:S(2)}) collective-permute-start(f32[32,18,1]{2,0,1:T(8,128)S(1)} %get-tuple-element.38), channel_id=1, source_target_pairs={{2,0},{3,1},{6,4},{7,5},{10,8},{11,9},{14,12},{15,13},{18,16},{19,... | collective-permute-start | bytes 6920 | tf_op jit(solution)/shard_map/ppermute | solution.py:21
  32.3 10.6 %collective-permute-start.7 = (f32[32,18,1]{2,0,1:T(8,128)S(1)}, f32[32,18,1]{2,0,1:T(8,128)S(1)}, u32[]{:S(2)}, u32[]{:S(2)}) collective-permute-start(f32[32,18,1]{2,0,1:T(8,128)S(1)} %get-tuple-element.37), channel_id=1, source_target_pairs={{0,2},{1,3},{4,6},{5,7},{8,10},{9,11},{12,14},{13,15},{16,18},{17,... | collective-permute-start | bytes 6920 | tf_op jit(solution)/shard_map/ppermute | solution.py:20
  43.6 4.7 %collective-permute-start.8 = (f32[32,1,128]{2,0,1:T(8,128)S(1)}, f32[32,1,128]{2,0,1:T(8,128)S(1)}, u32[]{:S(2)}, u32[]{:S(2)}) collective-permute-start(f32[32,1,128]{2,0,1:T(8,128)S(1)} %get-tuple-element.49), channel_id=1, source_target_pairs={{0,1},{1,4},{4,5},{5,8},{8,9},{9,12},{12,13},{2,3},{3,6},{6,7},{7,... | collective-permute-start | bytes 49160 | tf_op jit(solution)/shard_map/ppermute | solution.py:20
  47.0 4.5 %collective-permute-start.9 = (f32[32,1,128]{2,0,1:T(8,128)S(1)}, f32[32,1,128]{2,0,1:T(8,128)S(1)}, u32[]{:S(2)}, u32[]{:S(2)}) collective-permute-start(f32[32,1,128]{2,0,1:T(8,128)S(1)} %get-tuple-element.50), channel_id=1, source_target_pairs={{1,0},{4,1},{5,4},{8,5},{9,8},{12,9},{13,12},{3,2},{6,3},{7,6},{10... | collective-permute-start | bytes 49160 | tf_op jit(solution)/shard_map/ppermute | solution.py:21
  51.7 10.1 %collective-permute-start.10 = (f32[32,18,1]{2,0,1:T(8,128)S(1)}, f32[32,18,1]{2,0,1:T(8,128)S(1)}, u32[]{:S(2)}, u32[]{:S(2)}) collective-permute-start(f32[32,18,1]{2,0,1:T(8,128)S(1)} %get-tuple-element.34), channel_id=1, source_target_pairs={{2,0},{3,1},{6,4},{7,5},{10,8},{11,9},{14,12},{15,13},{18,16},{19,... | collective-permute-start | bytes 6920 | tf_op jit(solution)/shard_map/ppermute | solution.py:21
  53.0 10.6 %collective-permute-start.11 = (f32[32,18,1]{2,0,1:T(8,128)S(1)}, f32[32,18,1]{2,0,1:T(8,128)S(1)}, u32[]{:S(2)}, u32[]{:S(2)}) collective-permute-start(f32[32,18,1]{2,0,1:T(8,128)S(1)} %get-tuple-element.33), channel_id=1, source_target_pairs={{0,2},{1,3},{4,6},{5,7},{8,10},{9,11},{12,14},{13,15},{16,18},{17,... | collective-permute-start | bytes 6920 | tf_op jit(solution)/shard_map/ppermute | solution.py:20
  64.2 4.7 %collective-permute-start.12 = (f32[32,1,128]{2,0,1:T(8,128)S(1)}, f32[32,1,128]{2,0,1:T(8,128)S(1)}, u32[]{:S(2)}, u32[]{:S(2)}) collective-permute-start(f32[32,1,128]{2,0,1:T(8,128)S(1)} %get-tuple-element.47), channel_id=1, source_target_pairs={{0,1},{1,4},{4,5},{5,8},{8,9},{9,12},{12,13},{2,3},{3,6},{6,7},{7,... | collective-permute-start | bytes 49160 | tf_op jit(solution)/shard_map/ppermute | solution.py:20
  67.7 4.8 %collective-permute-start.13 = (f32[32,1,128]{2,0,1:T(8,128)S(1)}, f32[32,1,128]{2,0,1:T(8,128)S(1)}, u32[]{:S(2)}, u32[]{:S(2)}) collective-permute-start(f32[32,1,128]{2,0,1:T(8,128)S(1)} %get-tuple-element.48), channel_id=1, source_target_pairs={{1,0},{4,1},{5,4},{8,5},{9,8},{12,9},{13,12},{3,2},{6,3},{7,6},{10... | collective-permute-start | bytes 49160 | tf_op jit(solution)/shard_map/ppermute | solution.py:21
  72.6 10.1 %collective-permute-start.14 = (f32[32,18,1]{2,0,1:T(8,128)S(1)}, f32[32,18,1]{2,0,1:T(8,128)S(1)}, u32[]{:S(2)}, u32[]{:S(2)}) collective-permute-start(f32[32,18,1]{2,0,1:T(8,128)S(1)} %get-tuple-element.30), channel_id=1, source_target_pairs={{2,0},{3,1},{6,4},{7,5},{10,8},{11,9},{14,12},{15,13},{18,16},{19,... | collective-permute-start | bytes 6920 | tf_op jit(solution)/shard_map/ppermute | solution.py:21
  73.9 10.6 %collective-permute-start.15 = (f32[32,18,1]{2,0,1:T(8,128)S(1)}, f32[32,18,1]{2,0,1:T(8,128)S(1)}, u32[]{:S(2)}, u32[]{:S(2)}) collective-permute-start(f32[32,18,1]{2,0,1:T(8,128)S(1)} %get-tuple-element.29), channel_id=1, source_target_pairs={{0,2},{1,3},{4,6},{5,7},{8,10},{9,11},{12,14},{13,15},{16,18},{17,... | collective-permute-start | bytes 6920 | tf_op jit(solution)/shard_map/ppermute | solution.py:20
  85.1 4.7 %collective-permute-start.16 = (f32[32,1,128]{2,0,1:T(8,128)S(1)}, f32[32,1,128]{2,0,1:T(8,128)S(1)}, u32[]{:S(2)}, u32[]{:S(2)}) collective-permute-start(f32[32,1,128]{2,0,1:T(8,128)S(1)} %get-tuple-element.45), channel_id=1, source_target_pairs={{0,1},{1,4},{4,5},{5,8},{8,9},{9,12},{12,13},{2,3},{3,6},{6,7},{7,... | collective-permute-start | bytes 49160 | tf_op jit(solution)/shard_map/ppermute | solution.py:20
  88.6 4.0 %collective-permute-start.17 = (f32[32,1,128]{2,0,1:T(8,128)S(1)}, f32[32,1,128]{2,0,1:T(8,128)S(1)}, u32[]{:S(2)}, u32[]{:S(2)}) collective-permute-start(f32[32,1,128]{2,0,1:T(8,128)S(1)} %get-tuple-element.46), channel_id=1, source_target_pairs={{1,0},{4,1},{5,4},{8,5},{9,8},{12,9},{13,12},{3,2},{6,3},{7,6},{10... | collective-permute-start | bytes 49160 | tf_op jit(solution)/shard_map/ppermute | solution.py:21
  92.8 10.1 %collective-permute-start.18 = (f32[32,18,1]{2,0,1:T(8,128)S(1)}, f32[32,18,1]{2,0,1:T(8,128)S(1)}, u32[]{:S(2)}, u32[]{:S(2)}) collective-permute-start(f32[32,18,1]{2,0,1:T(8,128)S(1)} %get-tuple-element.26), channel_id=1, source_target_pairs={{2,0},{3,1},{6,4},{7,5},{10,8},{11,9},{14,12},{15,13},{18,16},{19,... | collective-permute-start | bytes 6920 | tf_op jit(solution)/shard_map/ppermute | solution.py:21
  94.1 10.6 %collective-permute-start.19 = (f32[32,18,1]{2,0,1:T(8,128)S(1)}, f32[32,18,1]{2,0,1:T(8,128)S(1)}, u32[]{:S(2)}, u32[]{:S(2)}) collective-permute-start(f32[32,18,1]{2,0,1:T(8,128)S(1)} %get-tuple-element.25), channel_id=1, source_target_pairs={{0,2},{1,3},{4,6},{5,7},{8,10},{9,11},{12,14},{13,15},{16,18},{17,... | collective-permute-start | bytes 6920 | tf_op jit(solution)/shard_map/ppermute | solution.py:20
  105.3 4.7 %collective-permute-start.20 = (f32[32,1,128]{2,0,1:T(8,128)S(1)}, f32[32,1,128]{2,0,1:T(8,128)S(1)}, u32[]{:S(2)}, u32[]{:S(2)}) collective-permute-start(f32[32,1,128]{2,0,1:T(8,128)S(1)} %get-tuple-element.43), channel_id=1, source_target_pairs={{0,1},{1,4},{4,5},{5,8},{8,9},{9,12},{12,13},{2,3},{3,6},{6,7},{7,... | collective-permute-start | bytes 49160 | tf_op jit(solution)/shard_map/ppermute | solution.py:20
  108.7 3.1 %collective-permute-start.21 = (f32[32,1,128]{2,0,1:T(8,128)S(1)}, f32[32,1,128]{2,0,1:T(8,128)S(1)}, u32[]{:S(2)}, u32[]{:S(2)}) collective-permute-start(f32[32,1,128]{2,0,1:T(8,128)S(1)} %get-tuple-element.44), channel_id=1, source_target_pairs={{1,0},{4,1},{5,4},{8,5},{9,8},{12,9},{13,12},{3,2},{6,3},{7,6},{10... | collective-permute-start | bytes 49160 | tf_op jit(solution)/shard_map/ppermute | solution.py:21
  112.0 10.1 %collective-permute-start.22 = (f32[32,18,1]{2,0,1:T(8,128)S(1)}, f32[32,18,1]{2,0,1:T(8,128)S(1)}, u32[]{:S(2)}, u32[]{:S(2)}) collective-permute-start(f32[32,18,1]{2,0,1:T(8,128)S(1)} %get-tuple-element.22), channel_id=1, source_target_pairs={{2,0},{3,1},{6,4},{7,5},{10,8},{11,9},{14,12},{15,13},{18,16},{19,... | collective-permute-start | bytes 6920 | tf_op jit(solution)/shard_map/ppermute | solution.py:21
  113.3 10.6 %collective-permute-start.23 = (f32[32,18,1]{2,0,1:T(8,128)S(1)}, f32[32,18,1]{2,0,1:T(8,128)S(1)}, u32[]{:S(2)}, u32[]{:S(2)}) collective-permute-start(f32[32,18,1]{2,0,1:T(8,128)S(1)} %get-tuple-element.21), channel_id=1, source_target_pairs={{0,2},{1,3},{4,6},{5,7},{8,10},{9,11},{12,14},{13,15},{16,18},{17,... | collective-permute-start | bytes 6920 | tf_op jit(solution)/shard_map/ppermute | solution.py:20
  (1 other events, 21.8 us)
